TPU v7x, 32 devices: a whole 2x2x4 slice. The times are simulated.
32 devices in a mesh: dp: 4 (over y, x), tensor: 4 (over z), pipe: 2 (over core).
Axes of the slice: x: 2, y: 2, z: 4, core: 2. Of those that a mesh axis runs over, the one named last changes fastest.
Arguments:
- acts: bfloat16 [6144, 4096], P(('dp', 'pipe')), may hold values from -6 to 6
- grad_hidden: bfloat16 [6144, 14336], P(('dp', 'pipe'), 'tensor'), may hold values from -384 to 384
- token_count: int32 [8], P(('dp', 'pipe')), may hold values from 1 to 768, as said below
- hot_ids: int32 [4, 358], P('tensor'), may hold values from 0 to 3583, as said below
- block_owner: int32 [112, 1], P('tensor'), may hold values from 0 to 3; in each aligned block of 28 rows (0 to 27, 28 to 55, ...) at most 14 rows name the same one
- master_hot: float32 [1432, 4096], P('tensor', ('dp', 'pipe')), may hold values from -6 to 6
- moment_hot: float32 [1432, 4096], P('tensor', ('dp', 'pipe')), may hold values from -3 to 3
- second_hot: float32 [1432, 4096], P('tensor', ('dp', 'pipe')), may hold values from 0.1 to 100
Outputs:
- new_master: float32 [1432, 4096], P('tensor', ('dp', 'pipe'))
- new_moment: float32 [1432, 4096], P('tensor', ('dp', 'pipe'))
- new_second: float32 [1432, 4096], P('tensor', ('dp', 'pipe'))
- hot_weights: bfloat16 [1432, 4096], P('tensor', 'dp')
- cold_sectioning: bfloat16 [224, 4096, 128], P('tensor', ('dp', 'pipe'))
Inputs may be any that keep to these rules, and one draw needn't show every extreme that they name: `token_count`: each micro-batch has at least one live token, and some micro-batch has exactly 768. `hot_ids`: each row lists 358 different offsets. `block_owner`: within the 28 blocks of one tensor index, no owner is named more than 14 times.
All inputs are finite; a program needn't handle non-finite values.
Results may differ from a plain program's by a relative error of at most 0.015.
Values may be sent and summed in bfloat16 or wider, within the bound.
A program may use at most 128 MiB of HBM per device.

v0:
```python
import jax
import jax.numpy as jnp
from jax import lax
from jax.sharding import PartitionSpec as P

CB = 128


def adam_update(g_hot, master_hot, moment_hot, second_hot):
    new_moment = 0.9 * moment_hot + 0.1 * g_hot
    new_second = 0.95 * second_hot + 0.05 * g_hot * g_hot
    bias_one = 1.0 - 0.9**4
    bias_two = 1.0 - 0.95**4
    new_master = master_hot - 0.02 * (new_moment / bias_one) / (
        jnp.sqrt(new_second / bias_two) + 1e-08
    )
    return (new_master, new_moment, new_second)


def shards(
    acts, grad_hidden, token_count, hot_ids, block_owner, master_hot, moment_hot, second_hot
):
    tok_slots = acts.shape[0]
    width = grad_hidden.shape[1]
    hot_count = hot_ids.shape[1]
    row_count = master_hot.shape[1]
    tensors = lax.axis_size("tensor")
    blocks = width // CB
    slots = max(2, (2 * blocks + tensors - 1) // tensors)
    live = lax.broadcasted_iota(jnp.int32, (tok_slots, 1), 0) < token_count[0]
    masked = jnp.where(live, grad_hidden, jnp.zeros_like(grad_hidden))
    total = lax.psum(token_count.astype(jnp.float32)[0], ("dp", "pipe"))
    column = lax.broadcasted_iota(jnp.int32, (width, hot_count), 0)
    selector = column == hot_ids[0][None, :]
    hot_mask = jnp.any(selector, axis=1)
    contract = (((0,), (0,)), ((), ()))
    summed = lax.psum_scatter(
        lax.dot_general(acts, masked, contract, preferred_element_type=jnp.float32).astype(
            jnp.bfloat16
        ),
        ("dp", "pipe"),
        scatter_dimension=0,
        tiled=True,
    ).astype(jnp.float32)
    grad = summed / total
    g_hot = lax.dot_general(
        selector.astype(jnp.float32),
        grad,
        (((0,), (1,)), ((), ())),
        precision=lax.Precision.HIGHEST,
        preferred_element_type=jnp.float32,
    )
    cold = jnp.where(hot_mask[None, :], 0.0, grad).astype(jnp.bfloat16)
    new_master, new_moment, new_second = adam_update(g_hot, master_hot, moment_hot, second_hot)
    hot_weights = lax.all_gather(new_master.astype(jnp.bfloat16), "pipe", axis=1, tiled=True)
    owner = block_owner[:, 0]
    same = owner[:, None] == owner[None, :]
    index = lax.broadcasted_iota(jnp.int32, (blocks, blocks), 0)
    other = lax.broadcasted_iota(jnp.int32, (blocks, blocks), 1)
    slot = jnp.sum((same & (other < index)).astype(jnp.int32), axis=1)
    target = owner * slots + slot
    places = lax.broadcasted_iota(jnp.int32, (tensors * slots, blocks), 0)
    placing = (places == target[None, :]).astype(jnp.bfloat16)
    tiles = cold.reshape(row_count, blocks, CB)
    packed = jnp.einsum("pb,rbc->prc", placing, tiles, preferred_element_type=jnp.float32).astype(
        jnp.bfloat16
    )
    cold_sectioning = lax.all_to_all(packed, "tensor", split_axis=0, concat_axis=0, tiled=True)
    return (new_master, new_moment, new_second, hot_weights, cold_sectioning)


def solution(mesh):
    in_specs = (
        P(("dp", "pipe"), None),
        P(("dp", "pipe"), "tensor"),
        P(("dp", "pipe")),
        P("tensor", None),
        P("tensor", None),
        P("tensor", ("dp", "pipe")),
        P("tensor", ("dp", "pipe")),
        P("tensor", ("dp", "pipe")),
    )
    out_specs = (
        P("tensor", ("dp", "pipe")),
        P("tensor", ("dp", "pipe")),
        P("tensor", ("dp", "pipe")),
        P("tensor", "dp"),
        P("tensor", ("dp", "pipe"), None),
    )
    return jax.shard_map(shards, mesh=mesh, in_specs=in_specs, out_specs=out_specs, check_vma=False)
```

profile of v0, /device:TPU:0, one launch (start us, length us, event | category | flops | bytes accessed | tf_op | source)
XLA Modules:
  0.0 420.0 jit_solution(12818828667416519670)
XLA Ops:
  7.2 0.0 reduce-scatter.2.cloned.1.call-start
  7.9 30.3 %fusion = bf16[4096,3584]{0,1:T(8,128)(2,1)} fusion(bf16[768,4096]{1,0:T(8,128)(2,1)} %param.8, bf16[768,3584]{1,0:T(8,128)(2,1)} %param.9, pred[768]{0:T(1024)(128)(4,1)S(1)} %iota_compare_fusion.4), kind=kOutput, calls=%fused_computation.1 | convolution fusion | flops 22566010880 | bytes 41157376 | tf_op jit(solution)/shard_map/dot_general | solution.py:38
  38.1 0.0 copy-start
  38.1 0.0 copy-start.4
  38.1 0.0 reduce-scatter.2.cloned.1.call-update
  38.2 16.3 %psum.7 = f32[]{:T(128)} all-reduce(f32[]{:T(128)} %bitcast.2), channel_id=1, replica_groups=mesh['dp'=4,'tensor'=4,'pipe'=2] {'dp','pipe'}, use_global_device_ids=true, to_apply=%region_1.2 | all-reduce | flops 1 | bytes 8 | tf_op jit(solution)/shard_map/psum | solution.py:32
  54.4 0.0 copy-done
  54.4 0.0 copy-done.4
  54.4 0.2 convert_reduce_fusion
  54.6 0.7 fusion.3
  55.4 161.5 %reduce-scatter.2.cloned.1.call-done = bf16[512,3584]{0,1:T(8,128)(2,1)} async-done(((bf16[4096,3584]{0,1:T(8,128)(2,1)}), bf16[512,3584]{0,1:T(8,128)(2,1)}) %reduce-scatter.2.cloned.1.call-update) | async-done | bytes 3670032 | tf_op jit(solution)/shard_map/reduce_scatter | solution.py:37
  216.8 5.2 %select_convert_fusion = bf16[512,3584]{0,1:T(8,128)(2,1)} fusion(bf16[512,3584]{0,1:T(8,128)(2,1)} %reduce-scatter.2.cloned.1.call-done, f32[]{:T(128)} %psum.7, pred[3584]{0:T(1024)(128)(4,1)S(1)} %fusion.3), kind=kLoop, calls=%fused_computation.2 | loop fusion | flops 7340032 | bytes 7343620 | tf_op jit(solution)/shard_map/convert_element_type | solution.py:53
  222.0 7.7 %copy.17 = bf16[512,28,128]{2,1,0:T(8,128)(2,1)} copy(bf16[512,28,128]{0,2,1:T(8,128)(2,1)} %bitcast.13) | data formatting | bytes 7340032 | tf_op jit(solution)/shard_map/reshape | solution.py:64
  229.8 4.4 %convolution_convert_fusion.1 = bf16[56,512,128]{2,0,1:T(8,128)(2,1)S(1)} fusion(bf16[512,28,128]{2,1,0:T(8,128)(2,1)} %copy.17, s32[28]{0:T(128)S(1)} %multiply_add_fusion.1), kind=kOutput, calls=%fused_computation.4 | convolution fusion | flops 209192480 | bytes 11010160 | tf_op jit(solution)/shard_map/pb,rbc->prc/dot_general | solution.py:65
  234.1 4.9 %copy.18 = bf16[56,512,128]{2,1,0:T(8,128)(2,1)} copy(bf16[56,512,128]{2,0,1:T(8,128)(2,1)S(1)} %convolution_convert_fusion.1) | data formatting | bytes 14680064 | tf_op jit(solution)/shard_map/convert_element_type | solution.py:65
  239.0 5.8 %all-to-all-start = ((bf16[56,512,128]{2,1,0:T(8,128)(2,1)}), bf16[56,512,128]{2,1,0:T(8,128)(2,1)}, u32[]{:S(2)}, u32[]{:S(2)}) async-start(bf16[56,512,128]{2,1,0:T(8,128)(2,1)} %copy.18), calls=%async_computation.1 | async-start | bytes 14680064 | tf_op jit(solution)/shard_map/all_to_all | solution.py:68
  244.8 0.0 copy-done.1
  244.8 0.0 copy-done.2
  244.8 0.0 copy-done.3
  244.8 10.0 %fusion.14 = (bf16[358,512]{1,0:T(8,128)(2,1)S(1)}, f32[358,512]{1,0:T(8,128)}, f32[358,512]{1,0:T(8,128)}, f32[358,512]{1,0:T(8,128)}) fusion(f32[358,512]{1,0:T(8,128)S(1)} %copy-done.1, f32[358,512]{1,0:T(8,128)S(1)} %copy-done.2, f32[358,512]{1,0:T(8,128)S(1)} %copy-done.3, bf16[512,3584]{0,1:T(8,128)(2,1)} %reduce-scatter.2.cloned.1.call-done, ...), kind=kOutput, calls=%fused_computation.26 | convolution fusion | flops 7890530304 | bytes 8437148 | tf_op jit(solution)/shard_map/dot_general | solution.py:46
  254.8 2.3 all_gather.3
  257.1 148.2 %all-to-all-done = bf16[56,512,128]{2,1,0:T(8,128)(2,1)} async-done(((bf16[56,512,128]{2,1,0:T(8,128)(2,1)}), bf16[56,512,128]{2,1,0:T(8,128)(2,1)}, u32[]{:S(2)}, u32[]{:S(2)}) %all-to-all-start) | async-done | bytes 7340064 | tf_op jit(solution)/shard_map/all_to_all | solution.py:68
  405.3 0.9 copy.22
  406.2 7.0 %copy.23 = bf16[56,512,128]{2,1,0:T(8,128)(2,1)} copy(bf16[56,512,128]{2,1,0:T(8,128)(2,1)} %all-to-all-done) | data formatting | bytes 14680064
  (6 shorter events, 0.0 us)
Async XLA Ops:
  7.2 209.7 %reduce-scatter.2.cloned.1.call-start = ((), (), s32[]{:S(2)}) async-start(), calls=%async_computation.2 | async-start | bytes 33030144 | tf_op jit(solution)/shard_map/reduce_scatter | solution.py:37
  38.1 16.3 %copy-start = (s32[1,358]{1,0:T(1,128)S(1)}, s32[1,358]{1,0:T(1,128)}, u32[]{:S(2)}) copy-start(s32[1,358]{1,0:T(1,128)} %param.11) | copy-start | bytes 4300
  38.1 16.3 %copy-start.4 = (s32[28,1]{0,1:T(1,128)S(1)}, s32[28,1]{0,1:T(1,128)}, u32[]{:S(2)}) copy-start(s32[28,1]{0,1:T(1,128)} %param.12) | copy-start | bytes 340
  239.0 5.8 %copy-start.1 = (f32[358,512]{1,0:T(8,128)S(1)}, f32[358,512]{1,0:T(8,128)}, u32[]{:S(2)}) copy-start(f32[358,512]{1,0:T(8,128)} %param.13) | copy-start | bytes 2199556
  239.0 5.8 %copy-start.2 = (f32[358,512]{1,0:T(8,128)S(1)}, f32[358,512]{1,0:T(8,128)}, u32[]{:S(2)}) copy-start(f32[358,512]{1,0:T(8,128)} %param.14) | copy-start | bytes 2199556
  239.0 5.8 %copy-start.3 = (f32[358,512]{1,0:T(8,128)S(1)}, f32[358,512]{1,0:T(8,128)}, u32[]{:S(2)}) copy-start(f32[358,512]{1,0:T(8,128)} %param.15) | copy-start | bytes 2199556
  239.0 166.3 %all-to-all-start = ((bf16[56,512,128]{2,1,0:T(8,128)(2,1)}), bf16[56,512,128]{2,1,0:T(8,128)(2,1)}, u32[]{:S(2)}, u32[]{:S(2)}) async-start(bf16[56,512,128]{2,1,0:T(8,128)(2,1)} %copy.18), calls=%async_computation.1 | async-start | bytes 14680064 | tf_op jit(solution)/shard_map/all_to_all | solution.py:68
Sparse Core Ops, SparseCore 0:
  38.3 178.5 reduce-scatter.1
where the time goes:
time: 421 us; the launch traced here: 420 us
  waiting for transfers between devices  310 us (74%)
  matrix products  44.6 us (11%)
  local copies, waits for them, and re-layouts  20.5 us (5%)
  blocking collectives  18.6 us (4%)
  between operations  14.7 us (3%)
  other arithmetic  6.13 us (1%)
  starting transfers between devices  5.8 us (1%)
    reduce_scatter x1, waiting for transfers between devices, shards(): lax.psum_scatter(lax.dot_general(acts, masked, contract, preferred_elemen...  161 us
    all_to_all x1, waiting for transfers between devices, shards(): lax.all_to_all(packed, 'tensor', split_axis=0, concat_axis=0, tiled=True)  148 us
    dot_general x1, matrix products, shards(): lax.dot_general(acts, masked, contract, preferred_element_type=jnp.float32)  30.3 us
    psum x1, blocking collectives, shards(): total = lax.psum(token_count.astype(jnp.float32)[0], ('dp', 'pipe'))  16.3 us
    dot_general x1, matrix products, shards(): lax.dot_general(selector.astype(jnp.float32), grad, (((0,), (1,)), ((), (...  9.96 us
  transfers between devices with their start and end apart: 2, of which 2 were waited for; matrix products, arithmetic and copies ran while one was open for 3% of the time, Pallas kernels for 0%

commit v1 on v0

--- a/solution.py
+++ b/solution.py
@@ -1,9 +1,332 @@
+import functools
+
 import jax
 import jax.numpy as jnp
 from jax import lax
+from jax.experimental import pallas as pl
+from jax.experimental.pallas import tpu as pltpu
 from jax.sharding import PartitionSpec as P
 
 CB = 128
+GROUP = 8
+LAGS = (1, 2, 2)
+
+
+def fused(
+    sizes, tc_ref, place_ref, hid_ref, acts, gh, mst, mom, sec,
+    mst_out, mom_out, sec_out, hw_out, cs_out,
+    acts_v, gh_v, acts_t, select, keep, hot_acc, state, hw_v, slots_v,
+    recv_a, recv_b, recv_c, tiles, packed, count,
+    acts_sem, gh_sem, state_sem, count_sem, send_a, land_a, send_b, land_b, send_c, land_c,
+    z_send, z_land, hw_sem,
+):
+    chunks, pieces, w, tensors, slots, width = sizes
+    half = CB // 2
+    total_pieces = chunks * pieces
+    ring = slots_v.shape[0]
+    row_count = chunks * CB
+    lag_b = LAGS[0]
+    lag_c = lag_b + LAGS[1]
+    lag_d = lag_c + LAGS[2]
+    dp, tz, pp = lax.axis_index("dp"), lax.axis_index("tensor"), lax.axis_index("pipe")
+    y, x = dp // 2, dp % 2
+
+    def peer(qy, qx, qc):
+        return (((y + qy) % 2) * 2 + (x + qx) % 2, tz, (pp + qc) % 2)
+
+    def remote(src, dst, ssem, rsem, device):
+        return pltpu.make_async_remote_copy(
+            src_ref=src, dst_ref=dst, send_sem=ssem, recv_sem=rsem,
+            device_id=device, device_id_type=pl.DeviceIdType.MESH,
+        )
+
+    def acts_copy(c, o):
+        return pltpu.make_async_copy(
+            acts.at[:, pl.ds(pl.multiple_of(o * row_count + c * CB, CB), CB)],
+            acts_v.at[c, o], acts_sem.at[c, o],
+        )
+
+    def gh_copy(p):
+        return pltpu.make_async_copy(
+            gh.at[:, pl.ds(pl.multiple_of(p * w, CB), w)], gh_v.at[p], gh_sem.at[p]
+        )
+
+    state_in = [
+        pltpu.make_async_copy(r, state.at[k], state_sem.at[k])
+        for k, r in enumerate((mst, mom, sec))
+    ]
+    for o in range(GROUP):
+        acts_copy(0, o).start()
+    gh_copy(0).start()
+    for p in range(1, pieces):
+        gh_copy(p).start()
+    for c in range(1, chunks):
+        for o in range(GROUP):
+            acts_copy(c, o).start()
+    for cp in state_in:
+        cp.start()
+
+    count[0] = jnp.full((8, 128), tc_ref[0], jnp.int32).astype(jnp.float32)
+    barrier = pltpu.get_barrier_semaphore()
+    for q in range(1, GROUP):
+        pl.semaphore_signal(
+            barrier, inc=1, device_id=peer(q // 4, (q // 2) % 2, q % 2),
+            device_id_type=pl.DeviceIdType.MESH,
+        )
+    for d in range(1, tensors):
+        pl.semaphore_signal(
+            barrier, inc=1, device_id=(dp, (tz + d) % tensors, pp),
+            device_id_type=pl.DeviceIdType.MESH,
+        )
+    pl.semaphore_wait(barrier, GROUP - 1 + tensors - 1)
+
+    counts = [
+        remote(
+            count.at[0], count.at[q], count_sem.at[0, q], count_sem.at[1, q],
+            peer(q // 4, (q // 2) % 2, q % 2),
+        )
+        for q in range(1, GROUP)
+    ]
+    for cp in counts:
+        cp.start()
+
+    def copy_a(i, h):
+        return remote(
+            slots_v.at[i % ring, h, pl.ds(4, 4)], recv_a.at[i, h],
+            send_a.at[i, h], land_a.at[i, h], peer(0, 0, 1),
+        )
+
+    def copy_b(i, h):
+        return remote(
+            slots_v.at[i % ring, h, pl.ds(2, 2)], recv_b.at[i, h],
+            send_b.at[i, h], land_b.at[i, h], peer(h, 1 - h, 0),
+        )
+
+    def copy_c(i, h):
+        return remote(
+            slots_v.at[i % ring, h, 1], recv_c.at[i, h],
+            send_c.at[i, h], land_c.at[i, h], peer(1 - h, h, 0),
+        )
+
+    def z_copy(c, d):
+        return remote(
+            packed.at[c, pl.ds(((tz + d) % tensors) * slots, slots)],
+            cs_out.at[pl.ds(tz * slots, slots), pl.ds(c * CB, CB)],
+            z_send.at[c, d], z_land.at[c, d], (dp, (tz + d) % tensors, pp),
+        )
+
+    def z_own(c):
+        return pltpu.make_async_copy(
+            packed.at[c, pl.ds(tz * slots, slots)],
+            cs_out.at[pl.ds(tz * slots, slots), pl.ds(c * CB, CB)],
+            z_send.at[c, 0],
+        )
+
+    tok = acts_v.shape[2]
+    live = lax.broadcasted_iota(jnp.int32, (tok, CB), 0) < tc_ref[0]
+    tiles[tiles.shape[0] - 1] = jnp.zeros((CB, CB), tiles.dtype)
+
+    def multiply(i):
+        c, p = i // pieces, i % pieces
+
+        @pl.when(p == 0)
+        def _():
+            for o in range(GROUP):
+                acts_copy(c, o).wait()
+            for q in range(GROUP):
+                qc, q1, q0 = q // 4, (q // 2) % 2, q % 2
+                o = ((y + q0) % 2) * 4 + ((x + q1) % 2) * 2 + (pp + qc) % 2
+                v = jnp.where(live, acts_v[c, o].astype(jnp.float32), 0.0)
+                acts_t[pl.ds(q * CB, CB)] = v.T.astype(jnp.bfloat16)
+
+        @pl.when(c == 0)
+        def _():
+            gh_copy(p).wait()
+
+        def halfway(k, carry):
+            base = pl.multiple_of(k * 4 * CB, CB)
+            r = jnp.dot(
+                acts_t[pl.ds(base, 4 * CB)], gh_v[p], preferred_element_type=jnp.float32
+            ).astype(jnp.bfloat16)
+            for q in range(4):
+                a, b = q % 2, q // 2
+                slots_v[i % ring, 0, k * 4 + q] = r[q * CB : q * CB + half]
+                slots_v[i % ring, 1, k * 4 + a * 2 + b] = r[q * CB + half : (q + 1) * CB]
+            return carry
+
+        lax.fori_loop(0, 2, halfway, 0)
+        for h in range(2):
+            copy_a(i, h).start()
+
+    def prepare():
+        for p in range(pieces):
+            column = lax.broadcasted_iota(jnp.int32, (select.shape[1], w), 1) + p * w
+            hit = (column == hid_ref[...]).astype(jnp.float32)
+            select[p] = hit.astype(jnp.bfloat16)
+            keep[p] = jnp.broadcast_to(1.0 - jnp.max(hit, axis=0, keepdims=True), (8, w))
+        for cp in counts:
+            cp.wait()
+        for cp in state_in:
+            cp.wait()
+
+    f32 = jnp.float32
+
+    def step_b(i):
+        for h in range(2):
+            copy_a(i, h).wait()
+            for k in (2, 3, 0, 1):
+                slots_v[i % ring, h, k] = (
+                    slots_v[i % ring, h, k].astype(f32) + recv_a[i, h, k].astype(f32)
+                ).astype(jnp.bfloat16)
+            copy_b(i, h).start()
+
+    def step_c(i):
+        for h in range(2):
+            copy_b(i, h).wait()
+            for k in (1, 0):
+                slots_v[i % ring, h, k] = (
+                    slots_v[i % ring, h, k].astype(f32) + recv_b[i, h, k].astype(f32)
+                ).astype(jnp.bfloat16)
+            copy_c(i, h).start()
+
+    def step_d(i):
+        c, p = i // pieces, i % pieces
+        total = count[0]
+        for q in range(1, GROUP):
+            total = total + count[q]
+        total = total[0:1, 0:1]
+        parts = []
+        for h in range(2):
+            copy_c(i, h).wait()
+            s = slots_v[i % ring, h, 0].astype(f32) + recv_c[i, h].astype(f32)
+            cold = jnp.where(keep[p][0:1] > 0.5, s / total, 0.0).astype(jnp.bfloat16)
+            for b in range(w // CB):
+                tiles[p * (w // CB) + b, pl.ds(h * half, half)] = cold[:, b * CB : (b + 1) * CB]
+            parts.append(s.astype(jnp.bfloat16))
+        whole = jnp.concatenate(parts, axis=0)
+        g = lax.dot_general(
+            select[p], whole, (((1,), (1,)), ((), ())), preferred_element_type=f32
+        )
+
+        @pl.when(p == 0)
+        def _():
+            hot_acc[...] = g
+
+        @pl.when(p > 0)
+        def _():
+            hot_acc[...] = hot_acc[...] + g
+
+        @pl.when(p == pieces - 1)
+        def _():
+            def place(k, carry):
+                packed[c, k] = tiles[place_ref[k]]
+                return carry
+
+            lax.fori_loop(0, tensors * slots, place, 0)
+            for d in range(tensors - 1, 0, -1):
+                z_copy(c, d).start()
+            z_own(c).start()
+            cols = pl.ds(pl.multiple_of(c * CB, CB), CB)
+            out = adam_update(
+                hot_acc[...] / total, state[0, :, cols], state[1, :, cols], state[2, :, cols]
+            )
+            for k in range(3):
+                state[k, :, cols] = out[k]
+            hw_v[:, cols] = out[0].astype(jnp.bfloat16)
+
+    def body(i, carry):
+        @pl.when(i < total_pieces)
+        def _():
+            multiply(i)
+
+        @pl.when(i == 1)
+        def _():
+            prepare()
+
+        @pl.when((i >= lag_d) & (i < total_pieces + lag_d))
+        def _():
+            step_d(i - lag_d)
+
+        @pl.when((i >= lag_c) & (i < total_pieces + lag_c))
+        def _():
+            step_c(i - lag_c)
+
+        @pl.when((i >= lag_b) & (i < total_pieces + lag_b))
+        def _():
+            step_b(i - lag_b)
+
+        return carry
+
+    lax.fori_loop(0, total_pieces + lag_d, body, 0)
+
+    mine = hw_out.at[:, pl.ds(pl.multiple_of(pp * row_count, CB), row_count)]
+    swap = remote(hw_v, mine, hw_sem.at[0], hw_sem.at[1], peer(0, 0, 1))
+    swap.start()
+    outs = [
+        pltpu.make_async_copy(state.at[k], r, state_sem.at[k])
+        for k, r in enumerate((mst_out, mom_out, sec_out))
+    ]
+    outs.append(pltpu.make_async_copy(hw_v, mine, hw_sem.at[2]))
+    for cp in outs:
+        cp.start()
+    for cp in outs:
+        cp.wait()
+    swap.wait()
+    for c in range(chunks):
+        z_own(c).wait()
+        for d in range(tensors - 1, 0, -1):
+            z_copy(c, d).wait()
+
+
+def fused_call(tok, placing, hot_ids, acts, grad_hidden, master, moment, second, slots):
+    tensors = lax.axis_size("tensor")
+    t, width = grad_hidden.shape
+    hot, rows = master.shape
+    chunks = rows // CB
+    blocks = width // CB
+    per = 4 if blocks % 4 == 0 else 1
+    w = per * CB
+    pieces = blocks // per
+    n = chunks * pieces
+    half = CB // 2
+    bf16, f32 = jnp.bfloat16, jnp.float32
+    dma = pltpu.SemaphoreType.DMA
+    hbm = pl.BlockSpec(memory_space=pl.ANY)
+    smem = pl.BlockSpec(memory_space=pltpu.SMEM)
+    state = jax.ShapeDtypeStruct((hot, rows), f32)
+    return pl.pallas_call(
+        functools.partial(fused, (chunks, pieces, w, tensors, slots, width)),
+        out_shape=(
+            state, state, state,
+            jax.ShapeDtypeStruct((hot, 2 * rows), bf16),
+            jax.ShapeDtypeStruct((tensors * slots, rows, CB), bf16),
+        ),
+        in_specs=[smem, smem, pl.BlockSpec(memory_space=pltpu.VMEM)] + [hbm] * 5,
+        out_specs=(hbm,) * 5,
+        scratch_shapes=[
+            pltpu.VMEM((chunks, GROUP, t, CB), bf16),
+            pltpu.VMEM((pieces, t, w), bf16),
+            pltpu.VMEM((GROUP * CB, t), bf16),
+            pltpu.VMEM((pieces, hot, w), bf16),
+            pltpu.VMEM((pieces, 8, w), f32),
+            pltpu.VMEM((hot, CB), f32),
+            pltpu.VMEM((3, hot, rows), f32),
+            pltpu.VMEM((hot, rows), bf16),
+            pltpu.VMEM((sum(LAGS) + 1, 2, GROUP, half, w), bf16),
+            pltpu.VMEM((n, 2, 4, half, w), bf16),
+            pltpu.VMEM((n, 2, 2, half, w), bf16),
+            pltpu.VMEM((n, 2, half, w), bf16),
+            pltpu.VMEM((blocks + 1, CB, CB), bf16),
+            pltpu.VMEM((chunks, tensors * slots, CB, CB), bf16),
+            pltpu.VMEM((GROUP, 8, 128), f32),
+            dma((chunks, GROUP)), dma((pieces,)), dma((3,)), dma((2, GROUP)),
+            dma((n, 2)), dma((n, 2)), dma((n, 2)), dma((n, 2)), dma((n, 2)), dma((n, 2)),
+            dma((chunks, tensors)), dma((chunks, tensors)), dma((3,)),
+        ],
+        compiler_params=pltpu.CompilerParams(
+            collective_id=0, has_side_effects=True, vmem_limit_bytes=67043328
+        ),
+    )(tok, placing, hot_ids, acts, grad_hidden, master, moment, second)
 
 
 def adam_update(g_hot, master_hot, moment_hot, second_hot):
@@ -27,6 +350,20 @@
     tensors = lax.axis_size("tensor")
     blocks = width // CB
     slots = max(2, (2 * blocks + tensors - 1) // tensors)
+    if lax.axis_size("dp") == 4 and lax.axis_size("pipe") == 2 and row_count % CB == 0:
+        owner = block_owner[:, 0]
+        same = owner[:, None] == owner[None, :]
+        index = lax.broadcasted_iota(jnp.int32, (blocks, blocks), 0)
+        other = lax.broadcasted_iota(jnp.int32, (blocks, blocks), 1)
+        slot = jnp.sum((same & (other < index)).astype(jnp.int32), axis=1)
+        target = owner * slots + slot
+        places = lax.broadcasted_iota(jnp.int32, (tensors * slots, blocks), 0)
+        number = lax.broadcasted_iota(jnp.int32, (tensors * slots, blocks), 1)
+        from_block = jnp.min(jnp.where(places == target[None, :], number, blocks), axis=1)
+        return fused_call(
+            token_count, from_block, hot_ids.reshape(hot_count, 1), acts, grad_hidden,
+            master_hot, moment_hot, second_hot, slots,
+        )
     live = lax.broadcasted_iota(jnp.int32, (tok_slots, 1), 0) < token_count[0]
     masked = jnp.where(live, grad_hidden, jnp.zeros_like(grad_hidden))
     total = lax.psum(token_count.astype(jnp.float32)[0], ("dp", "pipe"))

time: 421 us -> 228 us (0.54)
  waiting for transfers between devices: 310 us -> 0 us
  Pallas kernels: 0 us -> 208 us
  matrix products: 44.6 us -> 0 us
  blocking collectives: 18.6 us -> 0 us
  between operations: 14.7 us -> 1.29 us
  starting transfers between devices: 5.8 us -> 0 us
    pallas_call x0 -> x1, Pallas kernels: none -> 208 us  [fused_call(): pl.pallas_call(functools.partial(fused, (chunks, pieces, w, tensors, slot...]
    reduce_scatter x1 -> x0, waiting for transfers between devices: 161 us -> none  [shards(): lax.psum_scatter(lax.dot_general(acts, masked, contract, preferred_elemen...]
    all_to_all x1 -> x0, waiting for transfers between devices: 148 us -> none  [shards(): lax.all_to_all(packed, 'tensor', split_axis=0, concat_axis=0, tiled=True)]
    dot_general x3 -> x0, matrix products: 44.6 us -> none  [the longest x1 30.3 us: shards(): lax.dot_general(acts, masked, contract, preferred_element_type=jnp.float32)]
    psum x1 -> x0, blocking collectives: 16.3 us -> none  [shards(): total = lax.psum(token_count.astype(jnp.float32)[0], ('dp', 'pipe'))]
    unnamed x12 -> x5, local copies, waits for them, and re-layouts: 7.87 us -> 15.1 us
    reshape x1, local copies, waits for them, and re-layouts: 7.75 us -> 1.49 us  [shards(): hot_ids.reshape(hot_count, 1)]
    all_to_all x1 -> x0, starting transfers between devices: 5.76 us -> none  [shards(): lax.all_to_all(packed, 'tensor', split_axis=0, concat_axis=0, tiled=True)]
  transfers between devices with their start and end apart: 2 -> 0, of which waited for: 2 -> 0; matrix products, arithmetic and copies ran while one was open for 3% -> 0% of each run, Pallas kernels for 0% -> 0%
where the time goes in v1:
time: 228 us
  Pallas kernels  208 us (91%)
  local copies, waits for them, and re-layouts  16.6 us (7%)
    pallas_call x1, Pallas kernels, fused_call(): pl.pallas_call(functools.partial(fused, (chunks, pieces, w, tensors, slot...  208 us
    unnamed x5, local copies, waits for them, and re-layouts  15.1 us

profile of v1, /device:TPU:0, one launch (start us, length us, event | category | flops | bytes accessed | tf_op | source)
XLA Modules:
  0.0 227.7 jit_solution(7777611838849992984)
XLA Ops:
  1.3 0.9 convert_reduce_fusion
  2.2 0.7 multiply_add_fusion
  2.9 0.6 select_reduce_fusion.place_ref
  3.5 1.5 copy.14.hid_ref
  4.9 207.7 %shard_map.119 = (f32[358,512]{1,0:T(8,128)}, f32[358,512]{1,0:T(8,128)}, f32[358,512]{1,0:T(8,128)}, bf16[358,1024]{1,0:T(8,128)(2,1)}, bf16[56,512,128]{2,1,0:T(8,128)(2,1)}) custom-call(s32[1]{0:T(128)S(6)} %copy.20.tc_ref, s32[56]{0:T(128)} %select_reduce_fusion.place_ref, s32[358,1]{1,0:T(8,128)} %copy.14.hid_ref, bf16[768,4096]{1,0:T(8,128)(2,1)} %acts.1, ...), custom_call_target="tpu_custom_call" | custom-call | tf_op jit(solution)/shard_map/pallas_call | solution.py:297
  212.6 2.0 copy.21
  214.7 2.0 copy.22
  216.7 2.0 copy.23
  218.7 2.0 copy.24
  220.7 7.0 %copy.25 = bf16[56,512,128]{2,1,0:T(8,128)(2,1)} copy(bf16[56,512,128]{2,1,0:T(8,128)(2,1)} %get-tuple-element.14) | data formatting | bytes 14680064

commit v2 on v1

--- a/solution.py
+++ b/solution.py
@@ -9,6 +9,8 @@
 
 CB = 128
 GROUP = 8
+ROWS = 64
+PER = 7
 LAGS = (1, 2, 2)
 
 
@@ -16,15 +18,15 @@
     sizes, tc_ref, place_ref, hid_ref, acts, gh, mst, mom, sec,
     mst_out, mom_out, sec_out, hw_out, cs_out,
     acts_v, gh_v, acts_t, select, keep, hot_acc, state, hw_v, slots_v,
-    recv_a, recv_b, recv_c, tiles, packed, count,
+    recv_a, recv_b, recv_c, tiles, sums, packed, count,
     acts_sem, gh_sem, state_sem, count_sem, send_a, land_a, send_b, land_b, send_c, land_c,
     z_send, z_land, hw_sem,
 ):
     chunks, pieces, w, tensors, slots, width = sizes
-    half = CB // 2
+    half = ROWS // 2
     total_pieces = chunks * pieces
     ring = slots_v.shape[0]
-    row_count = chunks * CB
+    row_count = chunks * ROWS
     lag_b = LAGS[0]
     lag_c = lag_b + LAGS[1]
     lag_d = lag_c + LAGS[2]
@@ -60,7 +62,7 @@
     gh_copy(0).start()
     for p in range(1, pieces):
         gh_copy(p).start()
-    for c in range(1, chunks):
+    for c in range(1, row_count // CB):
         for o in range(GROUP):
             acts_copy(c, o).start()
     for cp in state_in:
@@ -111,50 +113,48 @@
     def z_copy(c, d):
         return remote(
             packed.at[c, pl.ds(((tz + d) % tensors) * slots, slots)],
-            cs_out.at[pl.ds(tz * slots, slots), pl.ds(c * CB, CB)],
+            cs_out.at[pl.ds(tz * slots, slots), pl.ds(c * ROWS, ROWS)],
             z_send.at[c, d], z_land.at[c, d], (dp, (tz + d) % tensors, pp),
         )
 
     def z_own(c):
         return pltpu.make_async_copy(
             packed.at[c, pl.ds(tz * slots, slots)],
-            cs_out.at[pl.ds(tz * slots, slots), pl.ds(c * CB, CB)],
+            cs_out.at[pl.ds(tz * slots, slots), pl.ds(c * ROWS, ROWS)],
             z_send.at[c, 0],
         )
 
     tok = acts_v.shape[2]
     live = lax.broadcasted_iota(jnp.int32, (tok, CB), 0) < tc_ref[0]
-    tiles[tiles.shape[0] - 1] = jnp.zeros((CB, CB), tiles.dtype)
+    hot_acc[...] = jnp.zeros_like(hot_acc)
+    tiles[tiles.shape[0] - 1] = jnp.zeros((ROWS, CB), tiles.dtype)
 
     def multiply(i):
         c, p = i // pieces, i % pieces
 
-        @pl.when(p == 0)
+        @pl.when((p == 0) & (c % 2 == 0))
         def _():
             for o in range(GROUP):
-                acts_copy(c, o).wait()
+                acts_copy(c // 2, o).wait()
             for q in range(GROUP):
                 qc, q1, q0 = q // 4, (q // 2) % 2, q % 2
                 o = ((y + q0) % 2) * 4 + ((x + q1) % 2) * 2 + (pp + qc) % 2
-                v = jnp.where(live, acts_v[c, o].astype(jnp.float32), 0.0)
-                acts_t[pl.ds(q * CB, CB)] = v.T.astype(jnp.bfloat16)
+                v = jnp.where(live, acts_v[c // 2, o].astype(jnp.float32), 0.0)
+                v = v.T.astype(jnp.bfloat16)
+                acts_t[0, pl.ds(q * ROWS, ROWS)] = v[:ROWS]
+                acts_t[1, pl.ds(q * ROWS, ROWS)] = v[ROWS:]
 
         @pl.when(c == 0)
         def _():
             gh_copy(p).wait()
 
-        def halfway(k, carry):
-            base = pl.multiple_of(k * 4 * CB, CB)
-            r = jnp.dot(
-                acts_t[pl.ds(base, 4 * CB)], gh_v[p], preferred_element_type=jnp.float32
-            ).astype(jnp.bfloat16)
-            for q in range(4):
-                a, b = q % 2, q // 2
-                slots_v[i % ring, 0, k * 4 + q] = r[q * CB : q * CB + half]
-                slots_v[i % ring, 1, k * 4 + a * 2 + b] = r[q * CB + half : (q + 1) * CB]
-            return carry
-
-        lax.fori_loop(0, 2, halfway, 0)
+        r = jnp.dot(
+            acts_t[c % 2], gh_v[p], preferred_element_type=jnp.float32
+        ).astype(jnp.bfloat16)
+        for q in range(GROUP):
+            k, a, b = q // 4, q % 2, (q // 2) % 2
+            slots_v[i % ring, 0, q] = r[q * ROWS : q * ROWS + half]
+            slots_v[i % ring, 1, k * 4 + a * 2 + b] = r[q * ROWS + half : (q + 1) * ROWS]
         for h in range(2):
             copy_a(i, h).start()
 
@@ -195,26 +195,20 @@
         for q in range(1, GROUP):
             total = total + count[q]
         total = total[0:1, 0:1]
-        parts = []
         for h in range(2):
             copy_c(i, h).wait()
             s = slots_v[i % ring, h, 0].astype(f32) + recv_c[i, h].astype(f32)
             cold = jnp.where(keep[p][0:1] > 0.5, s / total, 0.0).astype(jnp.bfloat16)
             for b in range(w // CB):
                 tiles[p * (w // CB) + b, pl.ds(h * half, half)] = cold[:, b * CB : (b + 1) * CB]
-            parts.append(s.astype(jnp.bfloat16))
-        whole = jnp.concatenate(parts, axis=0)
-        g = lax.dot_general(
-            select[p], whole, (((1,), (1,)), ((), ())), preferred_element_type=f32
-        )
-
-        @pl.when(p == 0)
-        def _():
-            hot_acc[...] = g
-
-        @pl.when(p > 0)
-        def _():
-            hot_acc[...] = hot_acc[...] + g
+            sums[p, pl.ds((c % 2) * ROWS + h * half, half)] = s.astype(jnp.bfloat16)
+
+        @pl.when(c % 2 == 1)
+        def _():
+            g = lax.dot_general(
+                select[p], sums[p], (((1,), (1,)), ((), ())), preferred_element_type=f32
+            )
+            hot_acc[...] = jnp.where(p == 0, 0.0, hot_acc[...]) + g
 
         @pl.when(p == pieces - 1)
         def _():
@@ -226,7 +220,10 @@
             for d in range(tensors - 1, 0, -1):
                 z_copy(c, d).start()
             z_own(c).start()
-            cols = pl.ds(pl.multiple_of(c * CB, CB), CB)
+
+        @pl.when((p == pieces - 1) & (c % 2 == 1))
+        def _():
+            cols = pl.ds(pl.multiple_of((c // 2) * CB, CB), CB)
             out = adam_update(
                 hot_acc[...] / total, state[0, :, cols], state[1, :, cols], state[2, :, cols]
             )
@@ -278,17 +275,54 @@
             z_copy(c, d).wait()
 
 
+def hand_out(refs, outs, bufs, sems, splits):
+    jobs = []
+    for k in range(len(splits)):
+        size = bufs[k].shape[0] // splits[k]
+        for j in range(splits[k]):
+            part = pl.ds(j * size, size)
+            jobs.append((
+                pltpu.make_async_copy(refs[k].at[part], bufs[k].at[part], sems[k].at[0, j]),
+                pltpu.make_async_copy(bufs[k].at[part], outs[k].at[part], sems[k].at[1, j]),
+            ))
+    for load, _ in jobs:
+        load.start()
+    for load, store in jobs:
+        load.wait()
+        store.start()
+    for _, store in jobs:
+        store.wait()
+
+
+def hand_out_call(arrays, splits):
+    n = len(arrays)
+    hbm = pl.BlockSpec(memory_space=pl.ANY)
+
+    def kernel(*refs):
+        hand_out(refs[:n], refs[n : 2 * n], refs[2 * n : 3 * n], refs[3 * n :], splits)
+
+    return pl.pallas_call(
+        kernel,
+        out_shape=tuple(jax.ShapeDtypeStruct(a.shape, a.dtype) for a in arrays),
+        in_specs=[hbm] * n,
+        out_specs=(hbm,) * n,
+        scratch_shapes=[pltpu.VMEM(a.shape, a.dtype) for a in arrays]
+        + [pltpu.SemaphoreType.DMA((2, k)) for k in splits],
+        compiler_params=pltpu.CompilerParams(vmem_limit_bytes=67043328),
+    )(*arrays)
+
+
 def fused_call(tok, placing, hot_ids, acts, grad_hidden, master, moment, second, slots):
     tensors = lax.axis_size("tensor")
     t, width = grad_hidden.shape
     hot, rows = master.shape
-    chunks = rows // CB
+    chunks = rows // ROWS
     blocks = width // CB
-    per = 4 if blocks % 4 == 0 else 1
+    per = PER if blocks % PER == 0 else 1
     w = per * CB
     pieces = blocks // per
     n = chunks * pieces
-    half = CB // 2
+    half = ROWS // 2
     bf16, f32 = jnp.bfloat16, jnp.float32
     dma = pltpu.SemaphoreType.DMA
     hbm = pl.BlockSpec(memory_space=pl.ANY)
@@ -304,9 +338,9 @@
         in_specs=[smem, smem, pl.BlockSpec(memory_space=pltpu.VMEM)] + [hbm] * 5,
         out_specs=(hbm,) * 5,
         scratch_shapes=[
-            pltpu.VMEM((chunks, GROUP, t, CB), bf16),
+            pltpu.VMEM((rows // CB, GROUP, t, CB), bf16),
             pltpu.VMEM((pieces, t, w), bf16),
-            pltpu.VMEM((GROUP * CB, t), bf16),
+            pltpu.VMEM((2, GROUP * ROWS, t), bf16),
             pltpu.VMEM((pieces, hot, w), bf16),
             pltpu.VMEM((pieces, 8, w), f32),
             pltpu.VMEM((hot, CB), f32),
@@ -316,10 +350,11 @@
             pltpu.VMEM((n, 2, 4, half, w), bf16),
             pltpu.VMEM((n, 2, 2, half, w), bf16),
             pltpu.VMEM((n, 2, half, w), bf16),
-            pltpu.VMEM((blocks + 1, CB, CB), bf16),
-            pltpu.VMEM((chunks, tensors * slots, CB, CB), bf16),
+            pltpu.VMEM((blocks + 1, ROWS, CB), bf16),
+            pltpu.VMEM((pieces, CB, w), bf16),
+            pltpu.VMEM((chunks, tensors * slots, ROWS, CB), bf16),
             pltpu.VMEM((GROUP, 8, 128), f32),
-            dma((chunks, GROUP)), dma((pieces,)), dma((3,)), dma((2, GROUP)),
+            dma((rows // CB, GROUP)), dma((pieces,)), dma((3,)), dma((2, GROUP)),
             dma((n, 2)), dma((n, 2)), dma((n, 2)), dma((n, 2)), dma((n, 2)), dma((n, 2)),
             dma((chunks, tensors)), dma((chunks, tensors)), dma((3,)),
         ],
@@ -360,10 +395,11 @@
         places = lax.broadcasted_iota(jnp.int32, (tensors * slots, blocks), 0)
         number = lax.broadcasted_iota(jnp.int32, (tensors * slots, blocks), 1)
         from_block = jnp.min(jnp.where(places == target[None, :], number, blocks), axis=1)
-        return fused_call(
+        results = fused_call(
             token_count, from_block, hot_ids.reshape(hot_count, 1), acts, grad_hidden,
             master_hot, moment_hot, second_hot, slots,
         )
+        return hand_out_call(results, (1, 1, 1, 1, tensors))
     live = lax.broadcasted_iota(jnp.int32, (tok_slots, 1), 0) < token_count[0]
     masked = jnp.where(live, grad_hidden, jnp.zeros_like(grad_hidden))
     total = lax.psum(token_count.astype(jnp.float32)[0], ("dp", "pipe"))

time: 228 us -> 206 us (0.904)
  local copies, waits for them, and re-layouts: 16.6 us -> 1.49 us
  Pallas kernels: 208 us -> 200 us
    unnamed x5 -> x0, local copies, waits for them, and re-layouts: 15.1 us -> none
    pallas_call x1, Pallas kernels: 208 us -> 194 us  [fused_call(): pl.pallas_call(functools.partial(fused, (chunks, pieces, w, tensors, slot...]
    pallas_call x0 -> x1, Pallas kernels: none -> 6.81 us  [hand_out_call(): pl.pallas_call(kernel, out_shape=tuple((jax.ShapeDtypeStruct(a.shape, a.d...]
where the time goes in v2:
time: 206 us; the launch traced here: 205 us
  Pallas kernels  200 us (97%)
  other arithmetic  2.17 us (1%)
    pallas_call x1, Pallas kernels, fused_call(): pl.pallas_call(functools.partial(fused, (chunks, pieces, w, tensors, slot...  194 us
    pallas_call x1, Pallas kernels, hand_out_call(): pl.pallas_call(kernel, out_shape=tuple((jax.ShapeDtypeStruct(a.shape, a.d...  6.81 us

profile of v2, /device:TPU:0, one launch (start us, length us, event | category | flops | bytes accessed | tf_op | source)
XLA Modules:
  0.0 205.3 jit_solution(13599348980192449578)
XLA Ops:
  1.3 0.9 convert_reduce_fusion
  2.2 0.7 multiply_add_fusion
  2.9 0.6 select_reduce_fusion.place_ref
  3.5 1.5 copy.14.hid_ref
  4.9 193.5 %shard_map.119 = (f32[358,512]{1,0:T(8,128)}, f32[358,512]{1,0:T(8,128)}, f32[358,512]{1,0:T(8,128)}, bf16[358,1024]{1,0:T(8,128)(2,1)}, bf16[56,512,128]{2,1,0:T(8,128)(2,1)}) custom-call(s32[1]{0:T(128)S(6)} %copy.15.tc_ref, s32[56]{0:T(128)} %select_reduce_fusion.place_ref, s32[358,1]{1,0:T(8,128)} %copy.14.hid_ref, bf16[768,4096]{1,0:T(8,128)(2,1)} %acts.1, ...), custom_call_target="tpu_custom_call" | custom-call | tf_op jit(solution)/shard_map/pallas_call | solution.py:331
  198.5 6.8 %shard_map.120 = (f32[358,512]{1,0:T(8,128)}, f32[358,512]{1,0:T(8,128)}, f32[358,512]{1,0:T(8,128)}, bf16[358,1024]{1,0:T(8,128)(2,1)}, bf16[56,512,128]{2,1,0:T(8,128)(2,1)}) custom-call(f32[358,512]{1,0:T(8,128)} %get-tuple-element.10.refs_0_, f32[358,512]{1,0:T(8,128)} %get-tuple-element.11.refs_1_, f32[358,512]{1,0:T(8,128)} %get-tuple-element.12.refs_2_, ...), custom_call_target="tpu_custom_call" | custom-call | tf_op jit(solution)/shard_map/pallas_call | solution.py:304

commit v3 on v2

--- a/solution.py
+++ b/solution.py
@@ -9,8 +9,9 @@
 
 CB = 128
 GROUP = 8
-ROWS = 64
-PER = 7
+ROWS = 32
+SUB = CB // ROWS
+PER = 14
 LAGS = (1, 2, 2)
 
 
@@ -132,24 +133,24 @@
     def multiply(i):
         c, p = i // pieces, i % pieces
 
-        @pl.when((p == 0) & (c % 2 == 0))
+        @pl.when((p == 0) & (c % SUB == 0))
         def _():
             for o in range(GROUP):
-                acts_copy(c // 2, o).wait()
+                acts_copy(c // SUB, o).wait()
             for q in range(GROUP):
                 qc, q1, q0 = q // 4, (q // 2) % 2, q % 2
                 o = ((y + q0) % 2) * 4 + ((x + q1) % 2) * 2 + (pp + qc) % 2
-                v = jnp.where(live, acts_v[c // 2, o].astype(jnp.float32), 0.0)
+                v = jnp.where(live, acts_v[c // SUB, o].astype(jnp.float32), 0.0)
                 v = v.T.astype(jnp.bfloat16)
-                acts_t[0, pl.ds(q * ROWS, ROWS)] = v[:ROWS]
-                acts_t[1, pl.ds(q * ROWS, ROWS)] = v[ROWS:]
+                for u in range(SUB):
+                    acts_t[u, pl.ds(q * ROWS, ROWS)] = v[u * ROWS : (u + 1) * ROWS]
 
         @pl.when(c == 0)
         def _():
             gh_copy(p).wait()
 
         r = jnp.dot(
-            acts_t[c % 2], gh_v[p], preferred_element_type=jnp.float32
+            acts_t[c % SUB], gh_v[p], preferred_element_type=jnp.float32
         ).astype(jnp.bfloat16)
         for q in range(GROUP):
             k, a, b = q // 4, q % 2, (q // 2) % 2
@@ -201,9 +202,9 @@
             cold = jnp.where(keep[p][0:1] > 0.5, s / total, 0.0).astype(jnp.bfloat16)
             for b in range(w // CB):
                 tiles[p * (w // CB) + b, pl.ds(h * half, half)] = cold[:, b * CB : (b + 1) * CB]
-            sums[p, pl.ds((c % 2) * ROWS + h * half, half)] = s.astype(jnp.bfloat16)
-
-        @pl.when(c % 2 == 1)
+            sums[p, pl.ds((c % SUB) * ROWS + h * half, half)] = s.astype(jnp.bfloat16)
+
+        @pl.when(c % SUB == SUB - 1)
         def _():
             g = lax.dot_general(
                 select[p], sums[p], (((1,), (1,)), ((), ())), preferred_element_type=f32
@@ -221,9 +222,9 @@
                 z_copy(c, d).start()
             z_own(c).start()
 
-        @pl.when((p == pieces - 1) & (c % 2 == 1))
-        def _():
-            cols = pl.ds(pl.multiple_of((c // 2) * CB, CB), CB)
+        @pl.when((p == pieces - 1) & (c % SUB == SUB - 1))
+        def _():
+            cols = pl.ds(pl.multiple_of((c // SUB) * CB, CB), CB)
             out = adam_update(
                 hot_acc[...] / total, state[0, :, cols], state[1, :, cols], state[2, :, cols]
             )
@@ -340,7 +341,7 @@
         scratch_shapes=[
             pltpu.VMEM((rows // CB, GROUP, t, CB), bf16),
             pltpu.VMEM((pieces, t, w), bf16),
-            pltpu.VMEM((2, GROUP * ROWS, t), bf16),
+            pltpu.VMEM((SUB, GROUP * ROWS, t), bf16),
             pltpu.VMEM((pieces, hot, w), bf16),
             pltpu.VMEM((pieces, 8, w), f32),
             pltpu.VMEM((hot, CB), f32),

time: 206 us -> 199 us (0.966)
  Pallas kernels: 200 us -> 194 us
    pallas_call x1, Pallas kernels: 194 us -> 187 us  [fused_call(): pl.pallas_call(functools.partial(fused, (chunks, pieces, w, tensors, slot...]
where the time goes in v3:
time: 199 us; the launch traced here: 198 us
  Pallas kernels  194 us (97%)
  other arithmetic  2.17 us (1%)
    pallas_call x1, Pallas kernels, fused_call(): pl.pallas_call(functools.partial(fused, (chunks, pieces, w, tensors, slot...  187 us
    pallas_call x1, Pallas kernels, hand_out_call(): pl.pallas_call(kernel, out_shape=tuple((jax.ShapeDtypeStruct(a.shape, a.d...  6.81 us

profile of v3, /device:TPU:0, one launch (start us, length us, event | category | flops | bytes accessed | tf_op | source)
XLA Modules:
  0.0 198.5 jit_solution(3166773025265333064)
XLA Ops:
  1.3 0.9 convert_reduce_fusion
  2.2 0.7 multiply_add_fusion
  2.9 0.6 select_reduce_fusion.place_ref
  3.5 1.5 copy.14.hid_ref
  4.9 186.7 %shard_map.119 = (f32[358,512]{1,0:T(8,128)}, f32[358,512]{1,0:T(8,128)}, f32[358,512]{1,0:T(8,128)}, bf16[358,1024]{1,0:T(8,128)(2,1)}, bf16[56,512,128]{2,1,0:T(8,128)(2,1)}) custom-call(s32[1]{0:T(128)S(6)} %copy.15.tc_ref, s32[56]{0:T(128)} %select_reduce_fusion.place_ref, s32[358,1]{1,0:T(8,128)} %copy.14.hid_ref, bf16[768,4096]{1,0:T(8,128)(2,1)} %acts.1, ...), custom_call_target="tpu_custom_call" | custom-call | tf_op jit(solution)/shard_map/pallas_call | solution.py:332
  191.7 6.8 %shard_map.120 = (f32[358,512]{1,0:T(8,128)}, f32[358,512]{1,0:T(8,128)}, f32[358,512]{1,0:T(8,128)}, bf16[358,1024]{1,0:T(8,128)(2,1)}, bf16[56,512,128]{2,1,0:T(8,128)(2,1)}) custom-call(f32[358,512]{1,0:T(8,128)} %get-tuple-element.10.refs_0_, f32[358,512]{1,0:T(8,128)} %get-tuple-element.11.refs_1_, f32[358,512]{1,0:T(8,128)} %get-tuple-element.12.refs_2_, ...), custom_call_target="tpu_custom_call" | custom-call | tf_op jit(solution)/shard_map/pallas_call | solution.py:305
